TPU v7x, 512 devices: a whole 4x8x8 slice. The times are simulated.
512 devices in a mesh: lrow: 8 (over z), rcol: 16 (over x, y_lo, core), term: 4 (over y_hi).
Axes of the slice: x: 4, y: 8 (y_hi: 4, y_lo: 2; y = y_hi * 2 + y_lo), z: 8, core: 2. Of those that a mesh axis runs over, the one named last changes fastest.
Arguments:
- core_left: bfloat16 [256, 256, 128], P(None, 'rcol'), may hold values from -6 to 6
- core_right: bfloat16 [256, 256, 128], P('rcol', 'lrow'), may hold values from -0.03125 to 0.03125
- env_left: bfloat16 [20, 32, 256], P('term', 'lrow'), may hold values from -0.375 to 0.375
- env_right: bfloat16 [20, 256, 256], P('term'), may hold values from -0.375 to 0.375
- coef_left: float32 [20, 3, 128], P('term'), may hold values from -1.5 to 1.5
- coef_right: float32 [20, 3, 128], P('term'), may hold values from -1.5 to 1.5
- projected: bfloat16 [128, 32, 256, 128], P('term', 'lrow', 'rcol'), may hold values from -6 to 6
Outputs:
- residual: bfloat16 [128, 32, 256, 128], P('term', 'lrow', 'rcol')
All inputs are finite; a program needn't handle non-finite values.
Results may differ from a plain program's by a relative error of at most 0.012.
Values may be sent and summed in bfloat16 or wider, within the bound.
No kernel may reach another device: no remote copies, remote signals or barrier semaphores. Data moves between devices by JAX's collectives and lax.ppermute only.
A program may use at most 64 MiB of HBM per device.

v0:
```python
import jax
import jax.numpy as jnp
from jax import lax
from jax.sharding import PartitionSpec as P


def stencil_terms(field, coef):
    wide = field.astype(jnp.float32)
    zero = jnp.zeros_like(wide[..., :1])
    before = jnp.concatenate([zero, wide[..., :-1]], axis=-1)
    after = jnp.concatenate([wide[..., 1:], zero], axis=-1)
    scaled = coef[:, :, None, None, :]
    return scaled[:, 0] * wide[None] + scaled[:, 1] * before[None] + scaled[:, 2] * after[None]


def on_device(core_left, core_right, env_left, env_right, coef_left, coef_right, projected):
    left_field = stencil_terms(core_left, coef_left).astype(jnp.bfloat16)
    left_frame = jnp.einsum(
        "tpq,tqrs->trps", env_left, left_field, preferred_element_type=jnp.float32
    ).astype(jnp.bfloat16)
    left_frame = lax.all_gather(left_frame, "rcol", axis=1, tiled=True)
    right_block = lax.all_gather(core_right, "lrow", axis=1, tiled=True)
    right_field = stencil_terms(right_block, coef_right).astype(jnp.bfloat16)
    right_frame = jnp.einsum(
        "tbq,trqj->trbj", env_right, right_field, preferred_element_type=jnp.float32
    ).astype(jnp.bfloat16)
    partial_sum = jnp.einsum(
        "trai,trbj->jabi",
        left_frame,
        lax.all_to_all(right_frame, "rcol", split_axis=2, concat_axis=1, tiled=True),
        preferred_element_type=jnp.float32,
    )
    summed = lax.psum_scatter(
        partial_sum.astype(jnp.bfloat16), "term", scatter_dimension=0, tiled=True
    ).astype(jnp.float32)
    return (projected.astype(jnp.float32) - summed).astype(jnp.bfloat16)


def solution(mesh):
    return jax.shard_map(
        on_device,
        mesh=mesh,
        in_specs=(
            P(None, "rcol", None),
            P("rcol", "lrow", None),
            P("term", "lrow", None),
            P("term", None, None),
            P("term", None, None),
            P("term", None, None),
            P("term", "lrow", "rcol", None),
        ),
        out_specs=P("term", "lrow", "rcol", None),
        check_vma=False,
    )
```

profile of v0, /device:TPU:20, one launch (start us, length us, event | category | flops | bytes accessed | tf_op | source)
XLA Modules:
  0.0 234.9 jit_solution(17720216909429817425)
XLA Ops:
  7.4 0.0 copy-start
  7.4 0.0 all-gather.3.cloned.1.call-start
  7.4 0.7 all-gather.3.cloned.1.call-update
  8.1 0.8 fusion.24
  8.9 48.0 %all-gather.3.cloned.1.call-done = bf16[16,256,128]{2,1,0:T(8,128)(2,1)} async-done(((bf16[16,32,128]{2,1,0:T(8,128)(2,1)}), bf16[16,256,128]{2,1,0:T(8,128)(2,1)}) %all-gather.3.cloned.1.call-update) | async-done | bytes 1048592 | tf_op jit(solution)/shard_map/all_gather | solution.py:22
  56.9 3.4 %fusion.22 = (f32[16,256,127]{2,1,0:T(8,128)}, f32[16,256,127]{2,1,0:T(8,128)S(1)}) fusion(bf16[16,256,128]{2,1,0:T(8,128)(2,1)} %all-gather.3.cloned.1.call-done), kind=kLoop, calls=%fused_computation.29 | loop fusion | bytes 8323072 | tf_op jit(solution)/shard_map/slice | solution.py:10
  60.3 2.9 %copy.48 = f32[16,256,127]{1,2,0:T(8,128)} copy(f32[16,256,127]{2,1,0:T(8,128)} %get-tuple-element.7) | data formatting | bytes 4161536
  63.3 1.9 copy.49
  65.2 0.0 copy-start.2
  65.2 2.0 concatenate.12.clone
  67.1 0.3 copy-done.2
  67.4 1.5 concatenate.13.clone
  68.9 2.7 %copy.23 = f32[16,256,128]{1,2,0:T(8,128)} copy(bf16[16,256,128]{2,1,0:T(8,128)(2,1)} %all-gather.3.cloned.1.call-done) | data formatting | bytes 3145728 | tf_op jit(solution)/shard_map/convert_element_type | solution.py:8
  71.5 0.0 copy-done
  71.5 5.8 %convert_bitcast_fusion = bf16[5,16,256,128]{2,3,1,0:T(8,128)(2,1)} fusion(f32[16,256,128]{1,2,0:T(8,128)} %concatenate.13.clone, f32[5,128]{1,0:T(8,128)S(1)} %get-tuple-element.15, f32[16,256,128]{1,2,0:T(8,128)S(1)} %concatenate.12.clone, f32[5,128]{1,0:T(8,128)S(1)} %get-tuple-element.16, f32[16,256,128]{1,2,0:T(8,128)} %copy.23, ...), kind=kOutput, calls=%fused_computation.5 | convolution fusion | flops 1360527360 | bytes 12197376 | tf_op jit(solution)/shard_map/tbq,trqj->trbj/dot_general | solution.py:24
  77.3 8.3 %copy.26 = bf16[5,16,256,128]{3,1,0,2:T(8,128)(2,1)} copy(bf16[5,16,256,128]{2,3,1,0:T(8,128)(2,1)} %convert_bitcast_fusion) | data formatting | bytes 10485760 | tf_op jit(solution)/shard_map/convert_element_type | solution.py:26
  85.6 0.0 copy-start.4
  85.6 0.0 copy-start.1
  85.6 5.9 %all-to-all-start = ((bf16[5,16,256,128]{3,1,0,2:T(8,128)(2,1)}), bf16[5,16,256,128]{3,1,0,2:T(8,128)(2,1)}, u32[]{:S(2)}, u32[]{:S(2)}) async-start(bf16[5,16,256,128]{3,1,0,2:T(8,128)(2,1)} %copy.26), calls=%async_computation | async-start | bytes 10485760 | tf_op jit(solution)/shard_map/all_to_all | solution.py:30
  91.5 0.0 all-gather.5.cloned.1.call-start
  91.5 0.0 copy-done.4
  91.6 0.0 copy-done.1
  91.6 0.2 copy.29
  91.8 0.4 fusion.21
  92.3 0.7 copy.50
  92.9 0.6 concatenate.14.clone
  93.6 0.0 copy-start.5
  93.6 0.7 copy.51
  94.2 0.2 concatenate.15.clone
  94.4 0.0 copy-done.5
  94.5 2.8 %fusion.18 = bf16[5,16,4,128]{3,2,1,0:T(4,128)(2,1)} fusion(f32[256,16,128]{2,0,1:T(8,128)S(1)} %concatenate.15.clone, f32[5,128]{1,0:T(8,128)S(1)} %get-tuple-element.17, f32[256,16,128]{2,0,1:T(8,128)S(1)} %concatenate.14.clone, f32[5,128]{1,0:T(8,128)S(1)} %get-tuple-element.18, f32[256,16,128]{2,0,1:T(8,128)S(1)} %copy.29, f32[5,128]{1,0:T(8,128)S(1)} %bitcast.50, ...), kind=kOutput, calls=%fused_computation.18 | convolution fusion | flops 36741120 | bytes 6391296 | tf_op jit(solution)/shard_map/tpq,tqrs->trps/dot_general | solution.py:18
  97.2 0.0 all-gather.5.cloned.1.call-update
  97.3 0.2 reduce-scatter.2.cloned.1.call-start
  97.5 56.7 %all-to-all-done = bf16[5,16,256,128]{3,1,0,2:T(8,128)(2,1)} async-done(((bf16[5,16,256,128]{3,1,0,2:T(8,128)(2,1)}), bf16[5,16,256,128]{3,1,0,2:T(8,128)(2,1)}, u32[]{:S(2)}, u32[]{:S(2)}) %all-to-all-start) | async-done | bytes 5242912 | tf_op jit(solution)/shard_map/all_to_all | solution.py:30
  154.2 6.2 %copy.28 = bf16[5,16,16,16,128]{4,3,2,1,0:T(8,128)(2,1)} copy(bf16[5,16,16,16,128]{4,2,0,3,1:T(8,128)(2,1)} %bitcast.6) | data formatting | bytes 10485760 | tf_op jit(solution)/shard_map/all_to_all | solution.py:30
  160.4 5.9 %all-gather.5.cloned.1.call-done = bf16[5,256,4,128]{3,2,1,0:T(4,128)(2,1)} async-done(((bf16[5,16,4,128]{3,2,1,0:T(4,128)(2,1)}), bf16[5,256,4,128]{3,2,1,0:T(4,128)(2,1)}) %all-gather.5.cloned.1.call-update) | async-done | bytes 1310736 | tf_op jit(solution)/shard_map/all_gather | solution.py:21
  166.3 0.0 copy-start.3
  166.3 7.7 %fusion.12 = bf16[128,4,16,128]{3,0,1,2:T(8,128)(2,1)} fusion(bf16[5,256,16,128,1]{3,2,1,0,4:T(8,128)(2,1)} %bitcast.46, bf16[5,256,4,128]{3,2,1,0:T(4,128)(2,1)} %all-gather.5.cloned.1.call-done), kind=kOutput, calls=%fused_computation.14 | convolution fusion | flops 2685403136 | bytes 8650752 | tf_op jit(solution)/shard_map/trai,trbj->jabi/dot_general | solution.py:27
  174.0 0.0 reduce-scatter.2.cloned.1.call-update
  174.0 50.9 %reduce-scatter.2.cloned.1.call-done = bf16[32,4,16,128]{3,0,1,2:T(8,128)(2,1)} async-done(((bf16[128,4,16,128]{3,0,1,2:T(8,128)(2,1)}), bf16[32,4,16,128]{3,0,1,2:T(8,128)(2,1)}) %reduce-scatter.2.cloned.1.call-update) | async-done | bytes 524304 | tf_op jit(solution)/shard_map/reduce_scatter | solution.py:33
  225.0 0.0 copy-done.3
  225.0 1.4 subtract_convert_fusion
  226.4 1.1 copy.34
  (5 shorter events, 0.0 us)
Async XLA Ops:
  7.4 64.2 %copy-start = (bf16[5,256,256]{2,1,0:T(8,128)(2,1)S(1)}, bf16[5,256,256]{2,1,0:T(8,128)(2,1)}, u32[]{:S(2)}) copy-start(bf16[5,256,256]{2,1,0:T(8,128)(2,1)} %param.10) | copy-start | bytes 1966084
  7.4 49.6 %all-gather.3.cloned.1.call-start = ((), (), s32[]{:S(2)}) async-start(), calls=%async_computation.2 | async-start | bytes 1179648 | tf_op jit(solution)/shard_map/all_gather | solution.py:22
  65.2 2.2 copy-start.2
  85.6 5.9 %copy-start.4 = (f32[5,3,128]{2,1,0:T(4,128)S(1)}, f32[5,3,128]{2,1,0:T(4,128)}, u32[]{:S(2)}) copy-start(f32[5,3,128]{2,1,0:T(4,128)} %param.11) | copy-start | bytes 23044
  85.6 6.0 %copy-start.1 = (bf16[256,16,128]{2,1,0:T(8,128)(2,1)S(1)}, bf16[256,16,128]{2,1,0:T(8,128)(2,1)}, u32[]{:S(2)}) copy-start(bf16[256,16,128]{2,1,0:T(8,128)(2,1)} %param.7) | copy-start | bytes 3145732
  85.6 68.6 %all-to-all-start = ((bf16[5,16,256,128]{3,1,0,2:T(8,128)(2,1)}), bf16[5,16,256,128]{3,1,0,2:T(8,128)(2,1)}, u32[]{:S(2)}, u32[]{:S(2)}) async-start(bf16[5,16,256,128]{3,1,0,2:T(8,128)(2,1)} %copy.26), calls=%async_computation | async-start | bytes 10485760 | tf_op jit(solution)/shard_map/all_to_all | solution.py:30
  91.5 74.9 %all-gather.5.cloned.1.call-start = ((), (), s32[]{:S(2)}) async-start(), calls=%async_computation.3 | async-start | bytes 1392640 | tf_op jit(solution)/shard_map/all_gather | solution.py:21
  93.6 0.9 copy-start.5
  97.3 127.7 %reduce-scatter.2.cloned.1.call-start = ((), (), s32[]{:S(2)}) async-start(), calls=%async_computation.4 | async-start | bytes 2621440 | tf_op jit(solution)/shard_map/reduce_scatter | solution.py:33
  166.3 58.6 %copy-start.3 = (bf16[32,4,16,128]{3,2,1,0:T(8,128)(2,1)S(1)}, bf16[32,4,16,128]{3,2,1,0:T(8,128)(2,1)}, u32[]{:S(2)}) copy-start(bf16[32,4,16,128]{3,2,1,0:T(8,128)(2,1)} %param.13) | copy-start | bytes 1572868
Sparse Core Ops, SparseCore 0:
  10.3 46.6 all-gather.2
  174.2 50.7 reduce-scatter.1
Sparse Core Ops, SparseCore 1:
  97.3 68.9 all-gather.4
where the time goes:
time: 235 us
  waiting for transfers between devices  162 us (69%)
  local copies, waits for them, and re-layouts  33.9 us (14%)
  matrix products  16.2 us (7%)
  between operations  15 us (6%)
  starting transfers between devices  6.14 us (3%)
    all_to_all x1, waiting for transfers between devices, on_device(): lax.all_to_all(right_frame, 'rcol', split_axis=2, concat_axis=1, tiled=True)  56.7 us
    reduce_scatter x1, waiting for transfers between devices, on_device(): lax.psum_scatter(partial_sum.astype(jnp.bfloat16), 'term', scatter_dimens...  50.9 us
    all_gather x1, waiting for transfers between devices, on_device(): right_block = lax.all_gather(core_right, 'lrow', axis=1, tiled=True)  48 us
    convert_element_type x1, local copies, waits for them, and re-layouts, on_device(): right_frame = jnp.einsum('tbq,trqj->trbj', env_right, right_field, prefer...  8.27 us
    dot_general x1, matrix products, on_device(): jnp.einsum('trai,trbj->jabi', left_frame, lax.all_to_all(right_frame, 'rc...  7.67 us
    unnamed x20, local copies, waits for them, and re-layouts  6.47 us
    all_to_all x1, local copies, waits for them, and re-layouts, on_device(): lax.all_to_all(right_frame, 'rcol', split_axis=2, concat_axis=1, tiled=True)  6.24 us
    all_gather x1, waiting for transfers between devices, on_device(): left_frame = lax.all_gather(left_frame, 'rcol', axis=1, tiled=True)  5.91 us
  transfers between devices with their start and end apart: 4, of which 4 were waited for; matrix products, arithmetic and copies ran while one was open for 5% of the time, Pallas kernels for 0%

commit v1 on v0

--- a/solution.py
+++ b/solution.py
@@ -2,6 +2,12 @@
 import jax.numpy as jnp
 from jax import lax
 from jax.sharding import PartitionSpec as P
+
+
+def tiled_gather(x, axis, dim):
+    devices = lax.axis_size(axis)
+    repeats = [devices if d == dim else 1 for d in range(x.ndim)]
+    return lax.all_to_all(jnp.tile(x, repeats), axis, split_axis=dim, concat_axis=dim, tiled=True)
 
 
 def stencil_terms(field, coef):
@@ -19,7 +25,7 @@
         "tpq,tqrs->trps", env_left, left_field, preferred_element_type=jnp.float32
     ).astype(jnp.bfloat16)
     left_frame = lax.all_gather(left_frame, "rcol", axis=1, tiled=True)
-    right_block = lax.all_gather(core_right, "lrow", axis=1, tiled=True)
+    right_block = tiled_gather(core_right, "lrow", 1)
     right_field = stencil_terms(right_block, coef_right).astype(jnp.bfloat16)
     right_frame = jnp.einsum(
         "tbq,trqj->trbj", env_right, right_field, preferred_element_type=jnp.float32

time: 235 us -> 225 us (0.957)
  the two profiles are of different devices: /device:TPU:20 before, /device:TPU:22 now
where the time goes in v1:
time: 225 us
  waiting for transfers between devices  140 us (62%)
  local copies, waits for them, and re-layouts  36.4 us (16%)
  starting transfers between devices  16.5 us (7%)
  matrix products  16.5 us (7%)
  between operations  13.6 us (6%)
    all_to_all x1, waiting for transfers between devices, on_device(): lax.all_to_all(right_frame, 'rcol', split_axis=2, concat_axis=1, tiled=True)  57.2 us
    reduce_scatter x1, waiting for transfers between devices, on_device(): lax.psum_scatter(partial_sum.astype(jnp.bfloat16), 'term', scatter_dimens...  51 us
    all_to_all x1, waiting for transfers between devices, tiled_gather(): lax.all_to_all(jnp.tile(x, repeats), axis, split_axis=dim, concat_axis=di...  28.7 us
    all_to_all x1, starting transfers between devices, tiled_gather(): lax.all_to_all(jnp.tile(x, repeats), axis, split_axis=dim, concat_axis=di...  10.3 us
    convert_element_type x1, local copies, waits for them, and re-layouts, on_device(): right_frame = jnp.einsum('tbq,trqj->trbj', env_right, right_field, prefer...  8.27 us
    dot_general x1, matrix products, on_device(): jnp.einsum('trai,trbj->jabi', left_frame, lax.all_to_all(right_frame, 'rc...  7.68 us
    unnamed x22, local copies, waits for them, and re-layouts  7.38 us
    all_to_all x1, local copies, waits for them, and re-layouts, on_device(): lax.all_to_all(right_frame, 'rcol', split_axis=2, concat_axis=1, tiled=True)  6.2 us
  transfers between devices with their start and end apart: 4, of which 4 were waited for; matrix products, arithmetic and copies ran while one was open for 5% of the time, Pallas kernels for 0%

profile of v1, /device:TPU:22, one launch (start us, length us, event | category | flops | bytes accessed | tf_op | source)
XLA Modules:
  0.0 224.5 jit_solution(13350860599251104618)
XLA Ops:
  6.5 0.0 copy-start
  6.5 0.0 copy-start.4
  6.5 1.1 tile.4
  7.7 1.7 copy.21
  9.4 10.3 %all-to-all-start = ((bf16[16,256,128]{2,0,1:T(8,128)(2,1)}), bf16[16,256,128]{2,0,1:T(8,128)(2,1)S(1)}, u32[]{:S(2)}, u32[]{:S(2)}) async-start(bf16[16,256,128]{2,0,1:T(8,128)(2,1)} %copy.21), calls=%async_computation | async-start | bytes 2097152 | tf_op jit(solution)/shard_map/all_to_all | solution.py:10
  19.7 0.0 copy-done.4
  19.7 28.7 %all-to-all-done = bf16[16,256,128]{2,0,1:T(8,128)(2,1)S(1)} async-done(((bf16[16,256,128]{2,0,1:T(8,128)(2,1)}), bf16[16,256,128]{2,0,1:T(8,128)(2,1)S(1)}, u32[]{:S(2)}, u32[]{:S(2)}) %all-to-all-start) | async-done | bytes 1048608 | tf_op jit(solution)/shard_map/all_to_all | solution.py:10
  48.4 2.5 %fusion.22 = (f32[16,256,127]{2,0,1:T(8,128)}, f32[16,256,127]{2,0,1:T(8,128)}) fusion(bf16[16,256,128]{2,0,1:T(8,128)(2,1)S(1)} %all-to-all-done), kind=kLoop, calls=%fused_computation.29 | loop fusion | bytes 8323072 | tf_op jit(solution)/shard_map/slice | solution.py:16
  50.9 2.9 %copy.47 = f32[16,256,127]{1,2,0:T(8,128)} copy(f32[16,256,127]{2,0,1:T(8,128)} %get-tuple-element.7) | data formatting | bytes 4161536
  53.8 3.0 %copy.48 = f32[16,256,127]{1,2,0:T(8,128)} copy(f32[16,256,127]{2,0,1:T(8,128)} %get-tuple-element.8) | data formatting | bytes 4161536
  56.9 0.0 copy-start.2
  56.9 3.3 %concatenate.12.clone = f32[16,256,128]{1,2,0:T(8,128)} pad(f32[16,256,127]{1,2,0:T(8,128)} %copy.47, f32[]{:T(128)} %constant.1.clone.1), padding=0_0x0_0x1_0 | pad | bytes 4177924 | tf_op jit(solution)/shard_map/concatenate | solution.py:16
  60.2 0.0 copy-done.2
  60.2 1.6 concatenate.13.clone
  61.7 1.8 copy.22
  63.5 0.0 copy-done
  63.5 6.1 %convert_bitcast_fusion = bf16[5,16,256,128]{2,3,1,0:T(8,128)(2,1)} fusion(f32[16,256,128]{1,2,0:T(8,128)} %concatenate.13.clone, f32[5,128]{1,0:T(8,128)S(1)} %get-tuple-element.15, f32[16,256,128]{1,2,0:T(8,128)} %concatenate.12.clone, f32[5,128]{1,0:T(8,128)S(1)} %get-tuple-element.16, f32[16,256,128]{1,2,0:T(8,128)} %copy.22, f32[5,128]{1,0:T(8,128)S(1)} %bitcast.49, ...), kind=kOutput, calls=%fused_computation.5 | convolution fusion | flops 1360527360 | bytes 12197376 | tf_op jit(solution)/shard_map/tbq,trqj->trbj/dot_general | solution.py:30
  69.6 8.3 %copy.25 = bf16[5,16,256,128]{3,1,0,2:T(8,128)(2,1)} copy(bf16[5,16,256,128]{2,3,1,0:T(8,128)(2,1)} %convert_bitcast_fusion) | data formatting | bytes 10485760 | tf_op jit(solution)/shard_map/convert_element_type | solution.py:32
  77.9 0.0 copy-start.5
  77.9 0.0 copy-start.1
  77.9 5.9 %all-to-all-start.1 = ((bf16[5,16,256,128]{3,1,0,2:T(8,128)(2,1)}), bf16[5,16,256,128]{3,1,0,2:T(8,128)(2,1)}, u32[]{:S(2)}, u32[]{:S(2)}) async-start(bf16[5,16,256,128]{3,1,0,2:T(8,128)(2,1)} %copy.25), calls=%async_computation.1 | async-start | bytes 10485760 | tf_op jit(solution)/shard_map/all_to_all | solution.py:36
  83.8 0.0 all-gather.2.cloned.1.call-start
  83.9 0.0 copy-done.5
  83.9 0.0 copy-done.1
  83.9 0.2 copy.28
  84.2 0.4 fusion.21
  84.6 0.7 copy.49
  85.3 0.6 concatenate.14.clone
  85.9 0.0 copy-start.6
  85.9 0.7 copy.50
  86.6 0.2 concatenate.15.clone
  86.8 0.0 copy-done.6
  86.8 2.8 %fusion.18 = bf16[5,16,4,128]{3,2,1,0:T(4,128)(2,1)} fusion(f32[256,16,128]{2,0,1:T(8,128)S(1)} %concatenate.15.clone, f32[5,128]{1,0:T(8,128)S(1)} %get-tuple-element.17, f32[256,16,128]{2,0,1:T(8,128)S(1)} %concatenate.14.clone, f32[5,128]{1,0:T(8,128)S(1)} %get-tuple-element.18, f32[256,16,128]{2,0,1:T(8,128)S(1)} %copy.28, f32[5,128]{1,0:T(8,128)S(1)} %bitcast.52, ...), kind=kOutput, calls=%fused_computation.18 | convolution fusion | flops 36741120 | bytes 6391296 | tf_op jit(solution)/shard_map/tpq,tqrs->trps/dot_general | solution.py:24
  89.6 0.0 all-gather.2.cloned.1.call-update
  89.6 0.2 reduce-scatter.2.cloned.1.call-start
  89.9 57.2 %all-to-all-done.1 = bf16[5,16,256,128]{3,1,0,2:T(8,128)(2,1)} async-done(((bf16[5,16,256,128]{3,1,0,2:T(8,128)(2,1)}), bf16[5,16,256,128]{3,1,0,2:T(8,128)(2,1)}, u32[]{:S(2)}, u32[]{:S(2)}) %all-to-all-start.1) | async-done | bytes 5242912 | tf_op jit(solution)/shard_map/all_to_all | solution.py:36
  147.0 6.2 %copy.27 = bf16[5,16,16,16,128]{4,3,2,1,0:T(8,128)(2,1)} copy(bf16[5,16,16,16,128]{4,2,0,3,1:T(8,128)(2,1)} %bitcast.7) | data formatting | bytes 10485760 | tf_op jit(solution)/shard_map/all_to_all | solution.py:36
  153.2 3.2 %all-gather.2.cloned.1.call-done = bf16[5,256,4,128]{3,2,1,0:T(4,128)(2,1)} async-done(((bf16[5,16,4,128]{3,2,1,0:T(4,128)(2,1)}), bf16[5,256,4,128]{3,2,1,0:T(4,128)(2,1)}) %all-gather.2.cloned.1.call-update) | async-done | bytes 1310736 | tf_op jit(solution)/shard_map/all_gather | solution.py:27
  156.4 0.0 copy-start.3
  156.4 7.7 %fusion.12 = bf16[128,4,16,128]{3,0,1,2:T(8,128)(2,1)} fusion(bf16[5,256,16,128,1]{3,2,1,0,4:T(8,128)(2,1)} %bitcast.47, bf16[5,256,4,128]{3,2,1,0:T(4,128)(2,1)} %all-gather.2.cloned.1.call-done), kind=kOutput, calls=%fused_computation.14 | convolution fusion | flops 2685403136 | bytes 8650752 | tf_op jit(solution)/shard_map/trai,trbj->jabi/dot_general | solution.py:33
  164.1 0.0 reduce-scatter.2.cloned.1.call-update
  164.1 51.0 %reduce-scatter.2.cloned.1.call-done = bf16[32,4,16,128]{3,0,1,2:T(8,128)(2,1)} async-done(((bf16[128,4,16,128]{3,0,1,2:T(8,128)(2,1)}), bf16[32,4,16,128]{3,0,1,2:T(8,128)(2,1)}) %reduce-scatter.2.cloned.1.call-update) | async-done | bytes 524304 | tf_op jit(solution)/shard_map/reduce_scatter | solution.py:39
  215.1 0.0 copy-done.3
  215.2 1.4 subtract_convert_fusion
  216.6 1.1 copy.33
  (6 shorter events, 0.0 us)
Async XLA Ops:
  6.5 57.0 %copy-start = (bf16[5,256,256]{2,1,0:T(8,128)(2,1)S(1)}, bf16[5,256,256]{2,1,0:T(8,128)(2,1)}, u32[]{:S(2)}) copy-start(bf16[5,256,256]{2,1,0:T(8,128)(2,1)} %param.10) | copy-start | bytes 1966084
  6.5 13.1 %copy-start.4 = (f32[5,3,128]{2,1,0:T(4,128)S(1)}, f32[5,3,128]{2,1,0:T(4,128)}, u32[]{:S(2)}) copy-start(f32[5,3,128]{2,1,0:T(4,128)} %param.12) | copy-start | bytes 23044
  9.4 39.0 %all-to-all-start = ((bf16[16,256,128]{2,0,1:T(8,128)(2,1)}), bf16[16,256,128]{2,0,1:T(8,128)(2,1)S(1)}, u32[]{:S(2)}, u32[]{:S(2)}) async-start(bf16[16,256,128]{2,0,1:T(8,128)(2,1)} %copy.21), calls=%async_computation | async-start | bytes 2097152 | tf_op jit(solution)/shard_map/all_to_all | solution.py:10
  56.9 3.3 %copy-start.2 = (f32[16,256,127]{1,2,0:T(8,128)S(1)}, f32[16,256,127]{1,2,0:T(8,128)}, u32[]{:S(2)}) copy-start(f32[16,256,127]{1,2,0:T(8,128)} %copy.48) | copy-start | bytes 6242308
  77.9 6.0 %copy-start.5 = (f32[5,3,128]{2,1,0:T(4,128)S(1)}, f32[5,3,128]{2,1,0:T(4,128)}, u32[]{:S(2)}) copy-start(f32[5,3,128]{2,1,0:T(4,128)} %param.11) | copy-start | bytes 23044
  77.9 6.0 %copy-start.1 = (bf16[256,16,128]{2,1,0:T(8,128)(2,1)S(1)}, bf16[256,16,128]{2,1,0:T(8,128)(2,1)}, u32[]{:S(2)}) copy-start(bf16[256,16,128]{2,1,0:T(8,128)(2,1)} %param.7) | copy-start | bytes 3145732
  77.9 69.1 %all-to-all-start.1 = ((bf16[5,16,256,128]{3,1,0,2:T(8,128)(2,1)}), bf16[5,16,256,128]{3,1,0,2:T(8,128)(2,1)}, u32[]{:S(2)}, u32[]{:S(2)}) async-start(bf16[5,16,256,128]{3,1,0,2:T(8,128)(2,1)} %copy.25), calls=%async_computation.1 | async-start | bytes 10485760 | tf_op jit(solution)/shard_map/all_to_all | solution.py:36
  83.8 72.6 %all-gather.2.cloned.1.call-start = ((), (), s32[]{:S(2)}) async-start(), calls=%async_computation.3 | async-start | bytes 1392640 | tf_op jit(solution)/shard_map/all_gather | solution.py:27
  85.9 0.9 copy-start.6
  89.6 125.5 %reduce-scatter.2.cloned.1.call-start = ((), (), s32[]{:S(2)}) async-start(), calls=%async_computation.4 | async-start | bytes 2621440 | tf_op jit(solution)/shard_map/reduce_scatter | solution.py:39
  156.4 58.7 %copy-start.3 = (bf16[32,4,16,128]{3,2,1,0:T(8,128)(2,1)S(1)}, bf16[32,4,16,128]{3,2,1,0:T(8,128)(2,1)}, u32[]{:S(2)}) copy-start(bf16[32,4,16,128]{3,2,1,0:T(8,128)(2,1)} %param.13) | copy-start | bytes 1572868
Sparse Core Ops, SparseCore 0:
  89.7 66.6 all-gather.1
  164.2 50.8 reduce-scatter.1
